TPU v7x, 32 devices: a whole 2x2x4 slice. The times are simulated.
32 devices in a mesh: dp: 8 (over z, core), fsdp: 4 (over y, x).
Axes of the slice: x: 2, y: 2, z: 4, core: 2. Of those that a mesh axis runs over, the one named last changes fastest.
Arguments:
- tokens: bfloat16 [32768, 768], P(('dp', 'fsdp')), may hold values from -6 to 6
- segments: int32 [32768], P(('dp', 'fsdp')), may hold values from -1 to 15, as said below
- cotangent: bfloat16 [32768, 768], P(('dp', 'fsdp')), may hold values from -6 to 6
- qkv_weight: bfloat16 [768, 2304], P('fsdp'), may hold values from -0.21875 to 0.21875
- qkv_bias: bfloat16 [2304], P('fsdp'), may hold values from -1.796875 to 1.796875
- out_weight: bfloat16 [768, 768], P('fsdp'), may hold values from -0.875 to 0.875
- out_bias: bfloat16 [768], P('fsdp'), may hold values from -1.796875 to 1.796875
- up_weight: bfloat16 [768, 3072], P('fsdp'), may hold values from -0.21875 to 0.21875
- up_bias: bfloat16 [3072], P('fsdp'), may hold values from -1.796875 to 1.796875
- down_weight: bfloat16 [3072, 768], P('fsdp'), may hold values from -0.109375 to 0.109375
- down_bias: bfloat16 [768], P('fsdp'), may hold values from -1.796875 to 1.796875
- first_gain: bfloat16 [768], P('fsdp'), may hold values from 0.5 to 1.5
- first_shift: bfloat16 [768], P('fsdp'), may hold values from -1.796875 to 1.796875
- second_gain: bfloat16 [768], P('fsdp'), may hold values from 0.5 to 1.5
- second_shift: bfloat16 [768], P('fsdp'), may hold values from -1.796875 to 1.796875
- query_gain: bfloat16 [64], P('fsdp'), may hold values from 0.099609375 to 1.8984375
- key_gain: bfloat16 [64], P('fsdp'), may hold values from 0.099609375 to 1.8984375
Outputs:
- out_tokens: bfloat16 [32768, 768], P(('dp', 'fsdp'))
- tokens_grad: bfloat16 [32768, 768], P(('dp', 'fsdp'))
- qkv_weight_grad: float32 [768, 2304], P('fsdp')
- qkv_bias_grad: float32 [2304], P('fsdp')
- out_weight_grad: float32 [768, 768], P('fsdp')
- out_bias_grad: float32 [768], P('fsdp')
- up_weight_grad: float32 [768, 3072], P('fsdp')
- up_bias_grad: float32 [3072], P('fsdp')
- down_weight_grad: float32 [3072, 768], P('fsdp')
- down_bias_grad: float32 [768], P('fsdp')
- first_gain_grad: float32 [768], P('fsdp')
- first_shift_grad: float32 [768], P('fsdp')
- second_gain_grad: float32 [768], P('fsdp')
- second_shift_grad: float32 [768], P('fsdp')
- query_gain_grad: float32 [64], P('fsdp')
- key_gain_grad: float32 [64], P('fsdp')
Inputs may be any that keep to these rules, and one draw needn't show every extreme that they name: `segments`: within each device's block of 1024 patches, equal ids mark one image; -1 marks padding, whose output and gradient vanish. Half of all blocks hold 4 sequences of four small images of 64 patches each; the others hold one sequence: an image of 576 patches, a second image, then padding.
All inputs are finite; a program needn't handle non-finite values.
Results may differ from a plain program's by a relative error of at most 0.024.
Values may be sent and summed in bfloat16 or wider, within the bound.
A program may use at most 256 MiB of HBM per device.

v0:
```python
import jax
import jax.numpy as jnp
from jax import lax
from jax.sharding import PartitionSpec as P

norm_eps = 1e-06


def layer_norm(value, gain, shift):
    centred = value - jnp.mean(value, axis=-1, keepdims=True)
    scaled = centred * lax.rsqrt(jnp.mean(centred * centred, axis=-1, keepdims=True) + norm_eps)
    return scaled * gain + shift


def head_scale(value, gain):
    centred = value - jnp.mean(value, axis=-1, keepdims=True)
    return (
        centred * lax.rsqrt(jnp.mean(centred * centred, axis=-1, keepdims=True) + norm_eps) * gain
    )


def head_norms(query, keys, query_gain, key_gain):
    return (head_scale(query, query_gain), head_scale(keys, key_gain))


def exact_gelu(value):
    return jax.nn.gelu(value, approximate=False)


def left_product(left, right):
    return lax.dot_general(
        left, right, (((0,), (0,)), ((), ())), preferred_element_type=jnp.float32
    )


def right_product(left, right):
    return lax.dot_general(
        left, right, (((1,), (1,)), ((), ())), preferred_element_type=jnp.float32
    )


def block_scores(query_block, key_low, segment_block, segments):
    scores = (
        jnp.einsum("qhe,khe->hqk", query_block, key_low, preferred_element_type=jnp.float32) * 0.125
    )
    allowed = segment_block[:, None] == segments[None, :]
    return jnp.where(allowed[None], scores, -1e30)


def attend(query_low, key_low, value_low, segments):
    count = query_low.shape[0]
    block = min(512, count)

    def one_block(position):
        query_block = lax.dynamic_slice_in_dim(query_low, position * block, block, 0)
        segment_block = lax.dynamic_slice_in_dim(segments, position * block, block, 0)
        scores = block_scores(query_block, key_low, segment_block, segments)
        top = jnp.max(scores, axis=-1, keepdims=True)
        expo = jnp.exp(scores - top)
        total = jnp.sum(expo, axis=-1, keepdims=True)
        weights = (expo / total).astype(jnp.bfloat16)
        attended = jnp.einsum(
            "hqk,khe->qhe", weights, value_low, preferred_element_type=jnp.float32
        )
        return (attended, (top + jnp.log(total))[..., 0])

    attended, log_total = lax.map(one_block, jnp.arange(count // block, dtype=jnp.int32))
    return (attended.reshape(query_low.shape), log_total)


def attend_back(query_low, key_low, value_low, segments, grad_attended, log_total):
    count = query_low.shape[0]
    block = min(512, count)

    def one_block(carry, item):
        key_grad, value_grad = carry
        position, block_total = item
        query_block = lax.dynamic_slice_in_dim(query_low, position * block, block, 0)
        segment_block = lax.dynamic_slice_in_dim(segments, position * block, block, 0)
        grad_block = lax.dynamic_slice_in_dim(grad_attended, position * block, block, 0)
        scores = block_scores(query_block, key_low, segment_block, segments)
        weights = jnp.exp(scores - block_total[..., None])
        value_grad = value_grad + jnp.einsum(
            "hqk,qhe->khe",
            weights.astype(jnp.bfloat16),
            grad_block,
            preferred_element_type=jnp.float32,
        )
        grad_weights = jnp.einsum(
            "qhe,khe->hqk", grad_block, value_low, preferred_element_type=jnp.float32
        )
        grad_scores = weights * (
            grad_weights - jnp.sum(weights * grad_weights, axis=-1, keepdims=True)
        )
        scores_low = grad_scores.astype(jnp.bfloat16)
        query_grad = 0.125 * jnp.einsum(
            "hqk,khe->qhe", scores_low, key_low, preferred_element_type=jnp.float32
        )
        key_grad = key_grad + 0.125 * jnp.einsum(
            "hqk,qhe->khe", scores_low, query_block, preferred_element_type=jnp.float32
        )
        return ((key_grad, value_grad), query_grad)

    empty = jnp.zeros(key_low.shape, jnp.float32)
    (key_grad, value_grad), query_grad = lax.scan(
        one_block, (empty, empty), (jnp.arange(count // block, dtype=jnp.int32), log_total)
    )
    return (query_grad.reshape(query_low.shape), key_grad, value_grad)


def shards(
    tokens,
    segments,
    cotangent,
    qkv_weight,
    qkv_bias,
    out_weight,
    out_bias,
    up_weight,
    up_bias,
    down_weight,
    down_bias,
    first_gain,
    first_shift,
    second_gain,
    second_shift,
    query_gain,
    key_gain,
):
    gathered = (
        lax.all_gather(qkv_weight, "fsdp", axis=0, tiled=True),
        lax.all_gather(qkv_bias, "fsdp", axis=0, tiled=True),
        lax.all_gather(out_weight, "fsdp", axis=0, tiled=True),
        lax.all_gather(out_bias, "fsdp", axis=0, tiled=True),
        lax.all_gather(up_weight, "fsdp", axis=0, tiled=True),
        lax.all_gather(up_bias, "fsdp", axis=0, tiled=True),
        lax.all_gather(down_weight, "fsdp", axis=0, tiled=True),
        lax.all_gather(down_bias, "fsdp", axis=0, tiled=True),
        lax.all_gather(first_gain, "fsdp", axis=0, tiled=True),
        lax.all_gather(first_shift, "fsdp", axis=0, tiled=True),
        lax.all_gather(second_gain, "fsdp", axis=0, tiled=True),
        lax.all_gather(second_shift, "fsdp", axis=0, tiled=True),
        lax.all_gather(query_gain, "fsdp", axis=0, tiled=True),
        lax.all_gather(key_gain, "fsdp", axis=0, tiled=True),
    )
    (
        qkv_matrix,
        qkv_offset,
        proj_matrix,
        proj_offset,
        up_matrix,
        up_offset,
        down_matrix,
        down_offset,
        gain_first,
        shift_first,
        gain_second,
        shift_second,
        gain_query,
        gain_key,
    ) = gathered
    count = tokens.shape[0]
    width = tokens.shape[1]
    head_size = gain_query.shape[0]
    heads = width // head_size
    float_tokens = tokens.astype(jnp.float32)
    normed_first, first_back = jax.vjp(
        layer_norm, float_tokens, gain_first.astype(jnp.float32), shift_first.astype(jnp.float32)
    )
    normed_low = normed_first.astype(jnp.bfloat16)
    mixed = jnp.dot(normed_low, qkv_matrix, preferred_element_type=jnp.float32) + qkv_offset.astype(
        jnp.float32
    )
    query = mixed[:, :width].reshape(count, heads, head_size)
    keys = mixed[:, width : 2 * width].reshape(count, heads, head_size)
    value_low = mixed[:, 2 * width :].reshape(count, heads, head_size).astype(jnp.bfloat16)
    (query_norm, key_norm), norm_back = jax.vjp(
        head_norms, query, keys, gain_query.astype(jnp.float32), gain_key.astype(jnp.float32)
    )
    query_low = query_norm.astype(jnp.bfloat16)
    key_low = key_norm.astype(jnp.bfloat16)
    attended, log_total = attend(query_low, key_low, value_low, segments)
    attended_low = attended.reshape(count, width).astype(jnp.bfloat16)
    residual = (
        float_tokens
        + jnp.dot(attended_low, proj_matrix, preferred_element_type=jnp.float32)
        + proj_offset.astype(jnp.float32)
    )
    normed_second, second_back = jax.vjp(
        layer_norm, residual, gain_second.astype(jnp.float32), shift_second.astype(jnp.float32)
    )
    second_low = normed_second.astype(jnp.bfloat16)
    hidden = jnp.dot(second_low, up_matrix, preferred_element_type=jnp.float32) + up_offset.astype(
        jnp.float32
    )
    active, gelu_back = jax.vjp(exact_gelu, hidden)
    active_low = active.astype(jnp.bfloat16)
    result = jnp.dot(
        active_low, down_matrix, preferred_element_type=jnp.float32
    ) + down_offset.astype(jnp.float32)
    valid = (segments >= 0)[:, None]
    output = jnp.where(valid, residual + result, 0.0).astype(jnp.bfloat16)
    weights_back = (
        lax.all_gather(qkv_weight, "fsdp", axis=0, tiled=True),
        lax.all_gather(qkv_bias, "fsdp", axis=0, tiled=True),
        lax.all_gather(out_weight, "fsdp", axis=0, tiled=True),
        lax.all_gather(out_bias, "fsdp", axis=0, tiled=True),
        lax.all_gather(up_weight, "fsdp", axis=0, tiled=True),
        lax.all_gather(up_bias, "fsdp", axis=0, tiled=True),
        lax.all_gather(down_weight, "fsdp", axis=0, tiled=True),
        lax.all_gather(down_bias, "fsdp", axis=0, tiled=True),
        lax.all_gather(first_gain, "fsdp", axis=0, tiled=True),
        lax.all_gather(first_shift, "fsdp", axis=0, tiled=True),
        lax.all_gather(second_gain, "fsdp", axis=0, tiled=True),
        lax.all_gather(second_shift, "fsdp", axis=0, tiled=True),
        lax.all_gather(query_gain, "fsdp", axis=0, tiled=True),
        lax.all_gather(key_gain, "fsdp", axis=0, tiled=True),
    )
    qkv_again = weights_back[0]
    proj_again = weights_back[2]
    up_again = weights_back[4]
    down_again = weights_back[6]
    grad_output = jnp.where(valid, cotangent.astype(jnp.float32), 0.0)
    result_low = grad_output.astype(jnp.bfloat16)
    down_grad = left_product(active_low, result_low)
    down_offset_grad = jnp.sum(result_low.astype(jnp.float32), axis=0)
    (grad_hidden,) = gelu_back(right_product(result_low, down_again))
    hidden_low = grad_hidden.astype(jnp.bfloat16)
    up_grad = left_product(second_low, hidden_low)
    up_offset_grad = jnp.sum(hidden_low.astype(jnp.float32), axis=0)
    grad_norm_second, second_gain_grad, second_shift_grad = second_back(
        right_product(hidden_low, up_again)
    )
    grad_residual = grad_output + grad_norm_second
    branch_low = grad_residual.astype(jnp.bfloat16)
    proj_grad = left_product(attended_low, branch_low)
    proj_offset_grad = jnp.sum(branch_low.astype(jnp.float32), axis=0)
    grad_attended = (
        right_product(branch_low, proj_again).astype(jnp.bfloat16).reshape(count, heads, head_size)
    )
    query_grad, key_grad, value_grad = attend_back(
        query_low, key_low, value_low, segments, grad_attended, log_total
    )
    grad_query, grad_keys, query_gain_grad, key_gain_grad = norm_back((query_grad, key_grad))
    grad_mixed = jnp.concatenate(
        [
            grad_query.reshape(count, width),
            grad_keys.reshape(count, width),
            value_grad.reshape(count, width),
        ],
        axis=1,
    ).astype(jnp.bfloat16)
    qkv_grad = left_product(normed_low, grad_mixed)
    qkv_offset_grad = jnp.sum(grad_mixed.astype(jnp.float32), axis=0)
    grad_norm_first, first_gain_grad, first_shift_grad = first_back(
        right_product(grad_mixed, qkv_again)
    )
    grad_input = (grad_residual + grad_norm_first).astype(jnp.bfloat16)
    summed = (
        lax.psum_scatter(
            qkv_grad.astype(jnp.bfloat16), "fsdp", scatter_dimension=0, tiled=True
        ).astype(jnp.float32),
        lax.psum_scatter(
            qkv_offset_grad.astype(jnp.bfloat16), "fsdp", scatter_dimension=0, tiled=True
        ).astype(jnp.float32),
        lax.psum_scatter(
            proj_grad.astype(jnp.bfloat16), "fsdp", scatter_dimension=0, tiled=True
        ).astype(jnp.float32),
        lax.psum_scatter(
            proj_offset_grad.astype(jnp.bfloat16), "fsdp", scatter_dimension=0, tiled=True
        ).astype(jnp.float32),
        lax.psum_scatter(
            up_grad.astype(jnp.bfloat16), "fsdp", scatter_dimension=0, tiled=True
        ).astype(jnp.float32),
        lax.psum_scatter(
            up_offset_grad.astype(jnp.bfloat16), "fsdp", scatter_dimension=0, tiled=True
        ).astype(jnp.float32),
        lax.psum_scatter(
            down_grad.astype(jnp.bfloat16), "fsdp", scatter_dimension=0, tiled=True
        ).astype(jnp.float32),
        lax.psum_scatter(
            down_offset_grad.astype(jnp.bfloat16), "fsdp", scatter_dimension=0, tiled=True
        ).astype(jnp.float32),
        lax.psum_scatter(
            first_gain_grad.astype(jnp.bfloat16), "fsdp", scatter_dimension=0, tiled=True
        ).astype(jnp.float32),
        lax.psum_scatter(
            first_shift_grad.astype(jnp.bfloat16), "fsdp", scatter_dimension=0, tiled=True
        ).astype(jnp.float32),
        lax.psum_scatter(
            second_gain_grad.astype(jnp.bfloat16), "fsdp", scatter_dimension=0, tiled=True
        ).astype(jnp.float32),
        lax.psum_scatter(
            second_shift_grad.astype(jnp.bfloat16), "fsdp", scatter_dimension=0, tiled=True
        ).astype(jnp.float32),
        lax.psum_scatter(
            query_gain_grad.astype(jnp.bfloat16), "fsdp", scatter_dimension=0, tiled=True
        ).astype(jnp.float32),
        lax.psum_scatter(
            key_gain_grad.astype(jnp.bfloat16), "fsdp", scatter_dimension=0, tiled=True
        ).astype(jnp.float32),
    )
    final = (
        lax.psum(summed[0].astype(jnp.bfloat16), "dp").astype(jnp.float32),
        lax.psum(summed[1].astype(jnp.bfloat16), "dp").astype(jnp.float32),
        lax.psum(summed[2].astype(jnp.bfloat16), "dp").astype(jnp.float32),
        lax.psum(summed[3].astype(jnp.bfloat16), "dp").astype(jnp.float32),
        lax.psum(summed[4].astype(jnp.bfloat16), "dp").astype(jnp.float32),
        lax.psum(summed[5].astype(jnp.bfloat16), "dp").astype(jnp.float32),
        lax.psum(summed[6].astype(jnp.bfloat16), "dp").astype(jnp.float32),
        lax.psum(summed[7].astype(jnp.bfloat16), "dp").astype(jnp.float32),
        lax.psum(summed[8].astype(jnp.bfloat16), "dp").astype(jnp.float32),
        lax.psum(summed[9].astype(jnp.bfloat16), "dp").astype(jnp.float32),
        lax.psum(summed[10].astype(jnp.bfloat16), "dp").astype(jnp.float32),
        lax.psum(summed[11].astype(jnp.bfloat16), "dp").astype(jnp.float32),
        lax.psum(summed[12].astype(jnp.bfloat16), "dp").astype(jnp.float32),
        lax.psum(summed[13].astype(jnp.bfloat16), "dp").astype(jnp.float32),
    )
    return (
        output,
        grad_input,
        final[0],
        final[1],
        final[2],
        final[3],
        final[4],
        final[5],
        final[6],
        final[7],
        final[8],
        final[9],
        final[10],
        final[11],
        final[12],
        final[13],
    )


def solution(mesh):
    in_specs = (
        P(("dp", "fsdp"), None),
        P(("dp", "fsdp")),
        P(("dp", "fsdp"), None),
        P("fsdp", None),
        P("fsdp"),
        P("fsdp", None),
        P("fsdp"),
        P("fsdp", None),
        P("fsdp"),
        P("fsdp", None),
        P("fsdp"),
        P("fsdp"),
        P("fsdp"),
        P("fsdp"),
        P("fsdp"),
        P("fsdp"),
        P("fsdp"),
    )
    out_specs = (
        P(("dp", "fsdp"), None),
        P(("dp", "fsdp"), None),
        P("fsdp", None),
        P("fsdp"),
        P("fsdp", None),
        P("fsdp"),
        P("fsdp", None),
        P("fsdp"),
        P("fsdp", None),
        P("fsdp"),
        P("fsdp"),
        P("fsdp"),
        P("fsdp"),
        P("fsdp"),
        P("fsdp"),
        P("fsdp"),
    )
    return jax.shard_map(shards, mesh=mesh, in_specs=in_specs, out_specs=out_specs, check_vma=False)
```

profile of v0, /device:TPU:0, one launch (start us, length us, event | category | flops | bytes accessed | tf_op | source)
XLA Modules:
  0.0 847.7 jit_solution(16748366694479090211)
XLA Ops:
  14.7 19.0 %all-reduce.22 = (bf16[2304]{0:T(1024)(128)(2,1)S(1)}, bf16[768]{0:T(1024)(128)(2,1)S(1)}, bf16[768]{0:T(1024)(128)(2,1)S(1)}, bf16[64]{0:T(256)(128)(2,1)S(1)},...) all-reduce(bf16[2304]{0:T(1024)(128)(2,1)S(1)} %dynamic-update-slic, ...), channel_id=1, replica_groups=mesh['dp'=8,'fsdp'=4] {'fsdp'}, use_global_device_ids=true, to_apply=%add.2 | all-reduce | flops 6272 | bytes 25088
  48.5 11.7 %all-gather.6.cloned.1.call-done = bf16[768,2304]{1,0:T(8,128)(2,1)} async-done(((bf16[192,2304]{1,0:T(8,128)(2,1)}), bf16[768,2304]{1,0:T(8,128)(2,1)}) %all-gather.6.cloned.1.call-update) | async-done | bytes 3538960 | tf_op jit(solution)/shard_map/all_gather | solution.py:131
  92.6 74.7 %while.27 = (s32[]{:T(128)}, bf16[2,512,12,64]{1,3,2,0:T(8,128)(2,1)}, f32[2,12,512]{2,1,0:T(8,128)S(1)}, s32[2]{0:T(128)S(1)}, s32[1024]{0:T(1024)S(1)}, /*inde...) while((s32[]{:T(128)}, ...), condition=%wide.region_9.10_spmd, body=%wide.region_6.9_spmd.sunk | while | flops 1686628352 | bytes 190286576 | solution.py:67
  94.6 11.5 %fusion.114 = (f32[12,512]{1,0:T(8,128)S(1)}, f32[12,512,1024]{2,1,0:T(8,128)}) fusion(pred[512,1024]{1,0:T(8,128)(4,1)S(1)} %broadcast_compare_fusion.5, bf16[1024,12,64]{0,2,1:T(8,128)(2,1)S(1)} %get-tuple-element.489, bf16[1024,12,64]{0,2,1:T(8,128)(2,1)S(1)} %get-tuple-element.488, s32[]{:T(128)S(6)} %select_n.77), kind=kOutput, calls=%fused_computation.3.clone.1 | convolution fusion | flops 824174592 | bytes 28073988 | tf_op jit(solution)/shard_map/while/body/eval_jaxpr/qhe,khe->hqk/dot_general | solution.py:44
  106.1 12.3 %fusion.115 = f32[12,512]{1,0:T(8,128)S(1)} fusion(f32[12,512,1024]{2,1,0:T(8,128)} %get-tuple-element.444, f32[12,512]{1,0:T(8,128)S(1)} %get-tuple-element.445, pred[512,1024]{1,0:T(8,128)(4,1)S(1)} %broadcast_compare_fusion.5), kind=kLoop, calls=%fused_computation.4.clone.1 | loop fusion | flops 25159680 | bytes 25739264 | tf_op jit(solution)/shard_map/while/body/eval_jaxpr/reduce_sum | solution.py:60
  132.1 10.7 %fusion.114 = (f32[12,512]{1,0:T(8,128)S(1)}, f32[12,512,1024]{2,1,0:T(8,128)}) fusion(pred[512,1024]{1,0:T(8,128)(4,1)S(1)} %broadcast_compare_fusion.5, bf16[1024,12,64]{0,2,1:T(8,128)(2,1)S(1)} %get-tuple-element.489, bf16[1024,12,64]{0,2,1:T(8,128)(2,1)S(1)} %get-tuple-element.488, s32[]{:T(128)S(6)} %select_n.77), kind=kOutput, calls=%fused_computation.3.clone.1 | convolution fusion | flops 824174592 | bytes 28073988 | tf_op jit(solution)/shard_map/while/body/eval_jaxpr/qhe,khe->hqk/dot_general | solution.py:44
  142.7 12.3 %fusion.115 = f32[12,512]{1,0:T(8,128)S(1)} fusion(f32[12,512,1024]{2,1,0:T(8,128)} %get-tuple-element.444, f32[12,512]{1,0:T(8,128)S(1)} %get-tuple-element.445, pred[512,1024]{1,0:T(8,128)(4,1)S(1)} %broadcast_compare_fusion.5), kind=kLoop, calls=%fused_computation.4.clone.1 | loop fusion | flops 25159680 | bytes 25739264 | tf_op jit(solution)/shard_map/while/body/eval_jaxpr/reduce_sum | solution.py:60
  188.7 38.1 %multiply_convert_fusion.1 = (bf16[1024,3072]{1,0:T(8,128)(2,1)}, f32[1024,3072]{1,0:T(8,128)}, f32[1024,3072]{1,0:T(8,128)}) fusion(f32[3072]{0:T(1024)S(1)} %bitcast.137, bf16[768,3072]{1,0:T(8,128)(2,1)} %all-gather.10.cloned.1.call-done, f32[1024,768]{0,1:T(8,128)} %copy-done.14, f32[768]{0:T(1024)S(1)} %copy-done.81, f32[768]{0:T(1024)S(1)} %copy-done.63, ...), kind=kOutput, calls=%fused_computation.40 | convolution fusion | flops 5043388416 | bytes 39348224 | tf_op jit(solution)/shard_map/dot_general | solution.py:193
  226.9 19.2 %fusion.72 = (bf16[3072]{0:T(1024)(128)(2,1)}, bf16[1024,3072]{1,0:T(8,128)(2,1)}) fusion(f32[1024,3072]{1,0:T(8,128)} %get-tuple-element.310, bf16[3072,768]{1,0:T(8,128)(2,1)} %all-gather.12.cloned.1.call-done, bf16[1024,768]{0,1:T(8,128)(2,1)} %copy.84, pred[1024]{0:T(1024)(128)(4,1)S(1)} %copy-done.69, f32[1024,3072]{1,0:T(8,128)} %get-tuple-element.326, ...), kind=kOutput, calls=%fused_computation.139 | convolution fusion | flops 4884526080 | bytes 37768192 | tf_op jit(solution)/shard_map/dot_general | solution.py:37
  246.1 10.3 %fusion.74 = (bf16[768]{0:T(1024)(128)(2,1)}, f32[1024,768]{1,0:T(8,128)}) fusion(bf16[1024,3072]{1,0:T(8,128)(2,1)} %get-tuple-element.328, bf16[768,3072]{1,0:T(8,128)(2,1)} %all-gather.10.cloned.1.call-done), kind=kOutput, calls=%fused_computation.141 | convolution fusion | flops 4832623616 | bytes 14157312 | tf_op jit(solution)/shard_map/dot_general | solution.py:37
  270.3 232.9 %while.28 = (s32[]{:T(128)}, f32[1024,12,64]{0,2,1:T(8,128)}, f32[1024,12,64]{0,2,1:T(8,128)}, f32[2,512,12,64]{1,0,3,2:T(2,128)}, s32[2]{0:T(128)S(1)}, /*index...) while((s32[]{:T(128)}, f32[1024,12,64]{0,2,1:T(8,128)}, ...), condition=%wide.region_16.17_spmd.clone, body=%wide.region_14.16_spmd.clone.sunk | while | flops 4125747200 | bytes 242411920 | solution.py:105
  282.7 18.3 %multiply_reduce_fusion.11 = (f32[12,512]{1,0:T(8,128)S(1)}, f32[12,512,1024]{2,1,0:T(8,128)}) fusion(f32[12,512,1024]{2,1,0:T(8,128)} %fusion.125, f32[12,512]{1,0:T(8,128)S(1)} %dynamic-slice_bitcast_fusion.2, pred[512,1024]{1,0:T(8,128)(4,1)S(1)} %broadcast_compare_fusion.6, bf16[1024,12,64]{0,2,1:T(8,128)(2,1)} %get-tuple-element.535, ...), kind=kOutput, calls=%fused_computation.15.clone.1 | convolution fusion | flops 836757504 | bytes 53264388 | tf_op jit(solution)/shard_map/while/body/eval_jaxpr/qhe,khe->hqk/dot_general | solution.py:89
  300.9 21.2 %multiply_convert_fusion.5 = bf16[12,512,1024]{2,1,0:T(8,128)(2,1)} fusion(f32[12,512,1024]{2,1,0:T(8,128)} %get-tuple-element.457, f32[12,512,1024]{2,1,0:T(8,128)} %fusion.125, f32[12,512]{1,0:T(8,128)S(1)} %get-tuple-element.458, f32[12,512]{1,0:T(8,128)S(1)} %dynamic-slice_bitcast_fusion.2, pred[512,1024]{1,0:T(8,128)(4,1)S(1)} %broadcast_compare_fusion.6), kind=kLoop, calls=%fused_computation.14.clone.1 | loop fusion | flops 37748736 | bytes 63488000 | tf_op jit(solution)/shard_map/while/body/eval_jaxpr/convert_element_type | solution.py:95
  334.9 28.8 %dynamic_update_slice.19 = f32[2,512,12,64]{1,0,3,2:T(2,128)} dynamic-update-slice(f32[2,512,12,64]{1,0,3,2:T(2,128)} %get-tuple-element.513, f32[1,512,12,64]{1,0,3,2:T(1,128)S(1)} %copy.132, s32[]{:T(128)} %get-tuple-element.510, s32[]{:T(128)} %constant.71.clone.1..sunk.1, s32[]{:T(128)} %constant.71.clone.1..sunk.1, s32[]{:T(128)} %constant.71.clone.1..sunk.1) | dynamic-update-slice | bytes 3145732 | tf_op jit(solution)/shard_map/while/body/jit(dynamic_update_index_in_dim)/dynamic_update_slice | solution.py:67
  372.6 13.4 %bitcast_add_fusion.5 = f32[1024,12,64]{0,2,1:T(8,128)} fusion(f32[1024,12,64]{0,2,1:T(8,128)} %get-tuple-element.512, f32[12,512,1024]{2,1,0:T(8,128)} %fusion.125, f32[12,512]{1,0:T(8,128)S(1)} %dynamic-slice_bitcast_fusion.2, pred[512,1024]{1,0:T(8,128)(4,1)S(1)} %copy-done.5, pred[]{:T(512)S(6)} %compare.3, ...), kind=kOutput, calls=%fused_computation.20.clone.1 | convolution fusion | flops 832045056 | bytes 32800772 | tf_op jit(solution)/shard_map/while/body/eval_jaxpr/hqk,qhe->khe/dot_general | solution.py:83
  398.0 18.3 %multiply_reduce_fusion.11 = (f32[12,512]{1,0:T(8,128)S(1)}, f32[12,512,1024]{2,1,0:T(8,128)}) fusion(f32[12,512,1024]{2,1,0:T(8,128)} %fusion.125, f32[12,512]{1,0:T(8,128)S(1)} %dynamic-slice_bitcast_fusion.2, pred[512,1024]{1,0:T(8,128)(4,1)S(1)} %broadcast_compare_fusion.6, bf16[1024,12,64]{0,2,1:T(8,128)(2,1)} %get-tuple-element.535, ...), kind=kOutput, calls=%fused_computation.15.clone.1 | convolution fusion | flops 836757504 | bytes 53264388 | tf_op jit(solution)/shard_map/while/body/eval_jaxpr/qhe,khe->hqk/dot_general | solution.py:89
  416.2 21.2 %multiply_convert_fusion.5 = bf16[12,512,1024]{2,1,0:T(8,128)(2,1)} fusion(f32[12,512,1024]{2,1,0:T(8,128)} %get-tuple-element.457, f32[12,512,1024]{2,1,0:T(8,128)} %fusion.125, f32[12,512]{1,0:T(8,128)S(1)} %get-tuple-element.458, f32[12,512]{1,0:T(8,128)S(1)} %dynamic-slice_bitcast_fusion.2, pred[512,1024]{1,0:T(8,128)(4,1)S(1)} %broadcast_compare_fusion.6), kind=kLoop, calls=%fused_computation.14.clone.1 | loop fusion | flops 37748736 | bytes 63488000 | tf_op jit(solution)/shard_map/while/body/eval_jaxpr/convert_element_type | solution.py:95
  450.1 28.8 %dynamic_update_slice.19 = f32[2,512,12,64]{1,0,3,2:T(2,128)} dynamic-update-slice(f32[2,512,12,64]{1,0,3,2:T(2,128)} %get-tuple-element.513, f32[1,512,12,64]{1,0,3,2:T(1,128)S(1)} %copy.132, s32[]{:T(128)} %get-tuple-element.510, s32[]{:T(128)} %constant.71.clone.1..sunk.1, s32[]{:T(128)} %constant.71.clone.1..sunk.1, s32[]{:T(128)} %constant.71.clone.1..sunk.1) | dynamic-update-slice | bytes 3145732 | tf_op jit(solution)/shard_map/while/body/jit(dynamic_update_index_in_dim)/dynamic_update_slice | solution.py:67
  488.7 14.3 %bitcast_add_fusion.5 = f32[1024,12,64]{0,2,1:T(8,128)} fusion(f32[1024,12,64]{0,2,1:T(8,128)} %get-tuple-element.512, f32[12,512,1024]{2,1,0:T(8,128)} %fusion.125, f32[12,512]{1,0:T(8,128)S(1)} %dynamic-slice_bitcast_fusion.2, pred[512,1024]{1,0:T(8,128)(4,1)S(1)} %copy-done.5, pred[]{:T(512)S(6)} %compare.3, ...), kind=kOutput, calls=%fused_computation.20.clone.1 | convolution fusion | flops 832045056 | bytes 32800772 | tf_op jit(solution)/shard_map/while/body/eval_jaxpr/hqk,qhe->khe/dot_general | solution.py:83
  619.3 14.8 %all-reduce.21 = (bf16[768]{0:T(1024)(128)(2,1)S(1)}, bf16[2304]{0:T(1024)(128)(2,1)S(1)}, bf16[768]{0:T(1024)(128)(2,1)S(1)}, bf16[3072]{0:T(1024)(128)(2,1)S(1...) all-reduce(bf16[768]{0:T(1024)(128)(2,1)S(1)} %dynamic-update-slice, ...), channel_id=1, replica_groups=mesh['dp'=8,'fsdp'=4] {'fsdp'}, use_global_device_ids=true, to_apply=%add.8 | all-reduce | flops 10880 | bytes 43520
  634.8 13.9 %all-reduce.19 = (bf16[576]{0:T(1024)(128)(2,1)S(1)}, bf16[192]{0:T(256)(128)(2,1)S(1)}, bf16[768]{0:T(1024)(128)(2,1)S(1)}, bf16[192]{0:T(256)(128)(2,1)S(1)}, ...) all-reduce(bf16[576]{0:T(1024)(128)(2,1)S(1)} %dynamic-slice.10, ...), channel_id=1, replica_groups=mesh['dp'=8,'fsdp'=4] {'dp'}, use_global_device_ids=true, to_apply=%region_27.28 | all-reduce | flops 2528 | bytes 10112 | tf_op jit(solution)/shard_map/psum | solution.py:305
  662.7 24.3 %reduce-scatter.9.cloned.1.call-done = bf16[192,3072]{1,0:T(8,128)(2,1)} async-done(((bf16[768,3072]{1,0:T(8,128)(2,1)}), bf16[192,3072]{1,0:T(8,128)(2,1)}) %reduce-scatter.9.cloned.1.call-update) | async-done | bytes 1179664 | tf_op jit(solution)/shard_map/reduce_scatter | solution.py:272
  687.0 60.0 %reduce-scatter.11.cloned.1.call-done = bf16[768,768]{1,0:T(8,128)(2,1)} async-done(((bf16[3072,768]{1,0:T(8,128)(2,1)}), bf16[768,768]{1,0:T(8,128)(2,1)}) %reduce-scatter.11.cloned.1.call-update) | async-done | bytes 1179664 | tf_op jit(solution)/shard_map/reduce_scatter | solution.py:278
  759.1 74.7 %all-reduce.25.cloned.1.call-done = (bf16[192,2304]{1,0:T(8,128)(2,1)}, bf16[192,768]{1,0:T(8,128)(2,1)}, bf16[192,3072]{1,0:T(8,128)(2,1)}, bf16[768,768]{1,0:T(8,128)(2,1)}) async-done(((bf16[192,2304]{1,0:T(8,128)(2,1)}, bf16[192,768]{1,0:T(8,128)(2,1)}, bf16[192,3072]{1,0:T(8,128)(2,1)}, bf16[768,768]{1,0:T(8,128)(2,1)}), (bf16[192,2304]{1,0:T(8,128)(2,1)}, bf16[192,768]{1,0:T(8,128)(2,1)}, ...) | async-done | bytes 3538960 | tf_op jit(solution)/shard_map/psum | solution.py:304
  (402 shorter events, 327.1 us)
Async XLA Ops:
  7.3 26.5 %copy-start.35 = (bf16[1024,768]{1,0:T(8,128)(2,1)S(1)}, bf16[1024,768]{1,0:T(8,128)(2,1)}, u32[]{:S(2)}) copy-start(bf16[1024,768]{1,0:T(8,128)(2,1)} %param.21) | copy-start | bytes 4718596
  7.3 52.9 %all-gather.6.cloned.1.call-start = ((), (), s32[]{:S(2)}) async-start(), calls=%async_computation.4 | async-start | bytes 4423680 | tf_op jit(solution)/shard_map/all_gather | solution.py:131
  8.0 163.9 %all-gather.8.cloned.1.call-start = ((), (), s32[]{:S(2)}) async-start(), calls=%async_computation.5 | async-start | bytes 1474560 | tf_op jit(solution)/shard_map/all_gather | solution.py:133
  8.8 179.9 %all-gather.10.cloned.1.call-start = ((), (), s32[]{:S(2)}) async-start(), calls=%async_computation.6 | async-start | bytes 5898240 | tf_op jit(solution)/shard_map/all_gather | solution.py:135
  9.5 217.4 %all-gather.12.cloned.1.call-start = ((), (), s32[]{:S(2)}) async-start(), calls=%async_computation.7 | async-start | bytes 5898240 | tf_op jit(solution)/shard_map/all_gather | solution.py:137
  10.1 652.6 %reduce-scatter.7.cloned.1.call-start = ((), (), s32[]{:S(2)}) async-start(), calls=%async_computation.9 | async-start | bytes 1474560 | tf_op jit(solution)/shard_map/reduce_scatter | solution.py:266
  33.7 26.4 %copy-start.53 = (f32[768]{0:T(1024)}, f32[768]{0:T(1024)S(1)}, u32[]{:S(2)}) copy-start(f32[768]{0:T(1024)S(1)} %convert_element_type.198) | copy-start | bytes 9220
  33.7 26.4 %copy-start.79 = (f32[768]{0:T(1024)}, f32[768]{0:T(1024)S(1)}, u32[]{:S(2)}) copy-start(f32[768]{0:T(1024)S(1)} %convert_element_type.199) | copy-start | bytes 9220
  34.5 25.6 %copy-start.11 = (bf16[1024,768]{0,1:T(8,128)(2,1)}, bf16[1024,768]{0,1:T(8,128)(2,1)S(1)}, u32[]{:S(2)}) copy-start(bf16[1024,768]{0,1:T(8,128)(2,1)S(1)} %copy.78) | copy-start | bytes 4718596
  34.8 31.6 %copy-start.51 = (f32[1024]{0:T(1024)}, f32[1024]{0:T(1024)S(1)}, u32[]{:S(2)}) copy-start(f32[1024]{0:T(1024)S(1)} %broadcast_multiply_fusion.3) | copy-start | bytes 12292
  35.3 31.1 %copy-start.57 = (f32[1024]{0:T(1024)}, f32[1024]{0:T(1024)S(1)}, u32[]{:S(2)}) copy-start(f32[1024]{0:T(1024)S(1)} %fusion.54) | copy-start | bytes 12292
  35.4 53.1 %copy-start.77 = (f32[64]{0:T(128)}, f32[64]{0:T(128)S(1)}, u32[]{:S(2)}) copy-start(f32[64]{0:T(128)S(1)} %convert_element_type.202) | copy-start | bytes 772
  35.4 53.1 %copy-start.71 = (f32[64]{0:T(128)}, f32[64]{0:T(128)S(1)}, u32[]{:S(2)}) copy-start(f32[64]{0:T(128)S(1)} %convert_element_type.204) | copy-start | bytes 772
  94.6 23.8 %copy-start.10 = (bf16[1024,12,64]{0,2,1:T(8,128)(2,1)S(1)}, bf16[1024,12,64]{0,2,1:T(8,128)(2,1)}, u32[]{:S(2)}) copy-start(bf16[1024,12,64]{0,2,1:T(8,128)(2,1)} %get-tuple-element.490) | copy-start | bytes 4718596 | tf_op jit(solution)/shard_map/while
  132.1 23.0 %copy-start.10 = (bf16[1024,12,64]{0,2,1:T(8,128)(2,1)S(1)}, bf16[1024,12,64]{0,2,1:T(8,128)(2,1)}, u32[]{:S(2)}) copy-start(bf16[1024,12,64]{0,2,1:T(8,128)(2,1)} %get-tuple-element.490) | copy-start | bytes 4718596 | tf_op jit(solution)/shard_map/while
  175.8 88.6 %copy-start.55 = (f32[1024]{0:T(1024)}, f32[1024]{0:T(1024)S(1)}, u32[]{:S(2)}) copy-start(f32[1024]{0:T(1024)S(1)} %broadcast_multiply_fusion.2) | copy-start | bytes 12292
  176.7 87.7 %copy-start.65 = (f32[1024]{0:T(1024)}, f32[1024]{0:T(1024)S(1)}, u32[]{:S(2)}) copy-start(f32[1024]{0:T(1024)S(1)} %fusion.55) | copy-start | bytes 12292
  188.7 38.2 %copy-start.69 = (pred[1024]{0:T(1024)(128)(4,1)S(1)}, pred[1024]{0:T(1024)(128)(4,1)}, u32[]{:S(2)}) copy-start(pred[1024]{0:T(1024)(128)(4,1)} %broadcast_compare_fusion.2) | copy-start | bytes 3076
  548.9 113.8 %reduce-scatter.5.cloned.1.call-start = ((), (), s32[]{:S(2)}) async-start(), calls=%async_computation.8 | async-start | bytes 4423680 | tf_op jit(solution)/shard_map/reduce_scatter | solution.py:260
  574.7 112.4 %reduce-scatter.9.cloned.1.call-start = ((), (), s32[]{:S(2)}) async-start(), calls=%async_computation.10 | async-start | bytes 5898240 | tf_op jit(solution)/shard_map/reduce_scatter | solution.py:272
  585.3 161.8 %reduce-scatter.11.cloned.1.call-start = ((), (), s32[]{:S(2)}) async-start(), calls=%async_computation.11 | async-start | bytes 5898240 | tf_op jit(solution)/shard_map/reduce_scatter | solution.py:278
  596.9 237.0 %all-reduce.25.cloned.1.call-start = ((), (), s32[]{:S(2)}) async-start(), calls=%async_computation.12 | async-start | bytes 7077888 | tf_op jit(solution)/shard_map/psum | solution.py:304
  617.9 36.4 %copy-start.60 = (f32[1024]{0:T(1024)S(1)}, f32[1024]{0:T(1024)}, u32[]{:S(2)}) copy-start(f32[1024]{0:T(1024)} %copy-done.59) | copy-start | bytes 12292
  660.0 87.1 %copy-start.16 = (f32[1024,768]{0,1:T(8,128)S(1)}, f32[1024,768]{0,1:T(8,128)}, u32[]{:S(2)}) copy-start(f32[1024,768]{0,1:T(8,128)} %copy-done.14) | copy-start | bytes 9437188
  (89 other events, 493.4 us)
Sparse Core Ops, SparseCore 0:
  9.9 50.1 all-gather.5
  62.0 27.5 all-gather.7
  91.4 56.9 all-gather.9
  150.1 56.9 all-gather.11
  549.1 27.3 reduce-scatter.6
  579.4 47.5 reduce-scatter.4
  630.0 57.0 reduce-scatter.8
  690.0 56.9 reduce-scatter.10
  749.7 84.1 all-reduce.24
where the time goes:
time: 856 us; the launch traced here: 848 us
  matrix products  291 us (34%)
  waiting for transfers between devices  173 us (20%)
  local copies, waits for them, and re-layouts  162 us (19%)
  other arithmetic  141 us (16%)
  blocking collectives  55.5 us (6%)
  between operations  20 us (2%)
    psum x1, waiting for transfers between devices, shards(): lax.psum(summed[0].astype(jnp.bfloat16), 'dp').astype(jnp.float32)  74.7 us
    dynamic_update_slice x4, local copies, waits for them, and re-layouts, attend(): lax.map(one_block, jnp.arange(count // block, dtype=jnp.int32))  63.6 us
    reduce_scatter x1, waiting for transfers between devices, shards(): lax.psum_scatter(down_grad.astype(jnp.bfloat16), 'fsdp', scatter_dimensio...  60 us
    convert_element_type x2, other arithmetic, one_block(): scores_low = grad_scores.astype(jnp.bfloat16)  42.4 us
    dot_general x4, matrix products, block_scores(): jnp.einsum('qhe,khe->hqk', query_block, key_low, preferred_element_type=j...  42.4 us
    dot_general x4, matrix products, right_product(): lax.dot_general(left, right, (((1,), (1,)), ((), ())), preferred_element_...  41.1 us
    dot_general x1, matrix products, shards(): jnp.dot(second_low, up_matrix, preferred_element_type=jnp.float32)  38.1 us
    dot_general x2, matrix products, one_block(): jnp.einsum('qhe,khe->hqk', grad_block, value_low, preferred_element_type=...  36.5 us
  transfers between devices with their start and end apart: 9, of which 4 were waited for; matrix products, arithmetic and copies ran while one was open for 30% of the time, Pallas kernels for 0%

commit v1 on v0

--- a/solution.py
+++ b/solution.py
@@ -301,7 +301,7 @@
         ).astype(jnp.float32),
     )
     final = (
-        lax.psum(summed[0].astype(jnp.bfloat16), "dp").astype(jnp.float32),
+        jnp.sum(lax.all_gather(summed[0].astype(jnp.bfloat16), "dp"), axis=0).astype(jnp.float32),
         lax.psum(summed[1].astype(jnp.bfloat16), "dp").astype(jnp.float32),
         lax.psum(summed[2].astype(jnp.bfloat16), "dp").astype(jnp.float32),
         lax.psum(summed[3].astype(jnp.bfloat16), "dp").astype(jnp.float32),

time: 856 us -> 806 us (0.942)
  waiting for transfers between devices: 173 us -> 123 us
    psum x1, waiting for transfers between devices: 74.7 us -> 0.01 us  [shards(): lax.psum(summed[2].astype(jnp.bfloat16), 'dp').astype(jnp.float32)]
    all_gather x0 -> x1, waiting for transfers between devices: none -> 61.2 us  [shards(): lax.all_gather(summed[0].astype(jnp.bfloat16), 'dp')]
    reduce_scatter x1, waiting for transfers between devices: 60 us -> 0.02 us  [shards(): lax.psum_scatter(down_grad.astype(jnp.bfloat16), 'fsdp', scatter_dimensio...]
    reduce_scatter x1, waiting for transfers between devices: 0.01 us -> 46.2 us  [shards(): lax.psum_scatter(qkv_grad.astype(jnp.bfloat16), 'fsdp', scatter_dimension...]
    reduce_scatter x1, waiting for transfers between devices: 24.3 us -> 0.02 us  [shards(): lax.psum_scatter(up_grad.astype(jnp.bfloat16), 'fsdp', scatter_dimension=...]
    unnamed x218 -> x220, local copies, waits for them, and re-layouts: 25.4 us -> 26.1 us
  transfers between devices with their start and end apart: 9 -> 10, of which waited for: 4 -> 3; matrix products, arithmetic and copies ran while one was open for 30% -> 66% of each run, Pallas kernels for 0% -> 0%
where the time goes in v1:
time: 806 us; the launch traced here: 797 us
  matrix products  293 us (36%)
  local copies, waits for them, and re-layouts  157 us (19%)
  other arithmetic  144 us (18%)
  waiting for transfers between devices  123 us (15%)
  blocking collectives  56.7 us (7%)
  between operations  20.2 us (3%)
    dynamic_update_slice x4, local copies, waits for them, and re-layouts, attend(): lax.map(one_block, jnp.arange(count // block, dtype=jnp.int32))  63.8 us
    all_gather x1, waiting for transfers between devices, shards(): lax.all_gather(summed[0].astype(jnp.bfloat16), 'dp')  61.2 us
    reduce_scatter x1, waiting for transfers between devices, shards(): lax.psum_scatter(qkv_grad.astype(jnp.bfloat16), 'fsdp', scatter_dimension...  46.2 us
    dot_general x4, matrix products, block_scores(): jnp.einsum('qhe,khe->hqk', query_block, key_low, preferred_element_type=j...  45.4 us
    convert_element_type x2, other arithmetic, one_block(): scores_low = grad_scores.astype(jnp.bfloat16)  44 us
    dot_general x4, matrix products, right_product(): lax.dot_general(left, right, (((1,), (1,)), ((), ())), preferred_element_...  42 us
    dot_general x1, matrix products, shards(): jnp.dot(second_low, up_matrix, preferred_element_type=jnp.float32)  38 us
    dot_general x2, matrix products, one_block(): jnp.einsum('qhe,khe->hqk', grad_block, value_low, preferred_element_type=...  36.9 us
  transfers between devices with their start and end apart: 10, of which 3 were waited for; matrix products, arithmetic and copies ran while one was open for 66% of the time, Pallas kernels for 0%

profile of v1, /device:TPU:0, one launch (start us, length us, event | category | flops | bytes accessed | tf_op | source)
XLA Modules:
  0.0 797.4 jit_solution(11015331963685651000)
XLA Ops:
  14.7 19.0 %all-reduce.22 = (bf16[2304]{0:T(1024)(128)(2,1)S(1)}, bf16[768]{0:T(1024)(128)(2,1)S(1)}, bf16[768]{0:T(1024)(128)(2,1)S(1)}, bf16[64]{0:T(256)(128)(2,1)S(1)},...) all-reduce(bf16[2304]{0:T(1024)(128)(2,1)S(1)} %dynamic-update-slic, ...), channel_id=1, replica_groups=mesh['dp'=8,'fsdp'=4] {'fsdp'}, use_global_device_ids=true, to_apply=%add.2 | all-reduce | flops 6272 | bytes 25088
  47.9 12.3 %all-gather.8.cloned.1.call-done = bf16[768,2304]{1,0:T(8,128)(2,1)} async-done(((bf16[192,2304]{1,0:T(8,128)(2,1)}), bf16[768,2304]{1,0:T(8,128)(2,1)}) %all-gather.8.cloned.1.call-update) | async-done | bytes 3538960 | tf_op jit(solution)/shard_map/all_gather | solution.py:131
  88.9 73.6 %while.27 = (s32[]{:T(128)}, bf16[2,512,12,64]{1,3,2,0:T(8,128)(2,1)}, f32[2,12,512]{2,1,0:T(8,128)S(1)}, s32[2]{0:T(128)S(1)}, s32[1024]{0:T(1024)S(1)}, /*inde...) while((s32[]{:T(128)}, ...), condition=%wide.region_9.10_spmd, body=%wide.region_6.9_spmd.sunk | while | flops 1686628352 | bytes 190286576 | solution.py:67
  90.8 11.5 %fusion.114 = (f32[12,512]{1,0:T(8,128)S(1)}, f32[12,512,1024]{2,1,0:T(8,128)}) fusion(pred[512,1024]{1,0:T(8,128)(4,1)S(1)} %broadcast_compare_fusion.5, bf16[1024,12,64]{0,2,1:T(8,128)(2,1)S(1)} %get-tuple-element.488, bf16[1024,12,64]{0,2,1:T(8,128)(2,1)S(1)} %get-tuple-element.487, s32[]{:T(128)S(6)} %select_n.77), kind=kOutput, calls=%fused_computation.3.clone.1 | convolution fusion | flops 824174592 | bytes 28073988 | tf_op jit(solution)/shard_map/while/body/eval_jaxpr/qhe,khe->hqk/dot_general | solution.py:44
  102.3 12.3 %fusion.115 = f32[12,512]{1,0:T(8,128)S(1)} fusion(f32[12,512,1024]{2,1,0:T(8,128)} %get-tuple-element.443, f32[12,512]{1,0:T(8,128)S(1)} %get-tuple-element.444, pred[512,1024]{1,0:T(8,128)(4,1)S(1)} %broadcast_compare_fusion.5), kind=kLoop, calls=%fused_computation.4.clone.1 | loop fusion | flops 25159680 | bytes 25739264 | tf_op jit(solution)/shard_map/while/body/eval_jaxpr/reduce_sum | solution.py:60
  127.9 10.7 %fusion.114 = (f32[12,512]{1,0:T(8,128)S(1)}, f32[12,512,1024]{2,1,0:T(8,128)}) fusion(pred[512,1024]{1,0:T(8,128)(4,1)S(1)} %broadcast_compare_fusion.5, bf16[1024,12,64]{0,2,1:T(8,128)(2,1)S(1)} %get-tuple-element.488, bf16[1024,12,64]{0,2,1:T(8,128)(2,1)S(1)} %get-tuple-element.487, s32[]{:T(128)S(6)} %select_n.77), kind=kOutput, calls=%fused_computation.3.clone.1 | convolution fusion | flops 824174592 | bytes 28073988 | tf_op jit(solution)/shard_map/while/body/eval_jaxpr/qhe,khe->hqk/dot_general | solution.py:44
  138.6 12.3 %fusion.115 = f32[12,512]{1,0:T(8,128)S(1)} fusion(f32[12,512,1024]{2,1,0:T(8,128)} %get-tuple-element.443, f32[12,512]{1,0:T(8,128)S(1)} %get-tuple-element.444, pred[512,1024]{1,0:T(8,128)(4,1)S(1)} %broadcast_compare_fusion.5), kind=kLoop, calls=%fused_computation.4.clone.1 | loop fusion | flops 25159680 | bytes 25739264 | tf_op jit(solution)/shard_map/while/body/eval_jaxpr/reduce_sum | solution.py:60
  172.9 38.0 %multiply_convert_fusion.1 = (bf16[1024,3072]{1,0:T(8,128)(2,1)}, f32[1024,3072]{1,0:T(8,128)}, f32[1024,3072]{1,0:T(8,128)}) fusion(f32[3072]{0:T(1024)S(1)} %bitcast.139, bf16[768,3072]{1,0:T(8,128)(2,1)} %all-gather.12.cloned.1.call-done, f32[1024,768]{0,1:T(8,128)S(1)} %get-tuple-element.324, f32[768]{0:T(1024)S(1)} %copy-done.80, ...), kind=kOutput, calls=%fused_computation.40 | convolution fusion | flops 5043388416 | bytes 39348224 | tf_op jit(solution)/shard_map/dot_general | solution.py:193
  210.9 19.4 %fusion.72 = (bf16[3072]{0:T(1024)(128)(2,1)}, bf16[1024,3072]{1,0:T(8,128)(2,1)}) fusion(f32[1024,3072]{1,0:T(8,128)} %get-tuple-element.309, bf16[3072,768]{1,0:T(8,128)(2,1)} %all-gather.14.cloned.1.call-done, bf16[1024,768]{0,1:T(8,128)(2,1)} %copy.84, pred[1024]{0:T(1024)(128)(4,1)S(1)} %copy-done.68, f32[1024,3072]{1,0:T(8,128)} %get-tuple-element.325, ...), kind=kOutput, calls=%fused_computation.139 | convolution fusion | flops 4884526080 | bytes 37768192 | tf_op jit(solution)/shard_map/dot_general | solution.py:37
  293.1 238.3 %while.28 = (s32[]{:T(128)}, f32[1024,12,64]{0,2,1:T(8,128)}, f32[1024,12,64]{0,2,1:T(8,128)}, f32[2,512,12,64]{1,0,3,2:T(2,128)}, s32[2]{0:T(128)S(1)}, /*index...) while((s32[]{:T(128)}, f32[1024,12,64]{0,2,1:T(8,128)}, ...), condition=%wide.region_16.17_spmd.clone, body=%wide.region_14.16_spmd.clone.sunk | while | flops 4125747200 | bytes 229828944 | solution.py:105
  294.8 11.8 %fusion.125 = f32[12,512,1024]{2,1,0:T(8,128)} fusion(bf16[1024,12,64]{0,2,1:T(8,128)(2,1)S(1)} %get-tuple-element.531, bf16[1024,12,64]{0,2,1:T(8,128)(2,1)} %get-tuple-element.529, s32[]{:T(128)S(6)} %select_n.81), kind=kOutput, calls=%fused_computation.28.clone.1 | convolution fusion | flops 805306368 | bytes 27525124 | tf_op jit(solution)/shard_map/while/body/eval_jaxpr/qhe,khe->hqk/dot_general | solution.py:44
  307.1 18.7 %multiply_reduce_fusion.11 = (f32[12,512]{1,0:T(8,128)S(1)}, f32[12,512,1024]{2,1,0:T(8,128)}) fusion(f32[12,512,1024]{2,1,0:T(8,128)} %fusion.125, f32[12,512]{1,0:T(8,128)S(1)} %dynamic-slice_bitcast_fusion.2, pred[512,1024]{1,0:T(8,128)(4,1)S(1)} %broadcast_compare_fusion.6, bf16[1024,12,64]{0,2,1:T(8,128)(2,1)} %get-tuple-element.534, ...), kind=kOutput, calls=%fused_computation.15.clone.1 | convolution fusion | flops 836757504 | bytes 53264388 | tf_op jit(solution)/shard_map/while/body/eval_jaxpr/qhe,khe->hqk/dot_general | solution.py:89
  325.8 22.7 %multiply_convert_fusion.5 = bf16[12,512,1024]{2,1,0:T(8,128)(2,1)} fusion(f32[12,512,1024]{2,1,0:T(8,128)} %get-tuple-element.456, f32[12,512,1024]{2,1,0:T(8,128)} %fusion.125, f32[12,512]{1,0:T(8,128)S(1)} %get-tuple-element.457, f32[12,512]{1,0:T(8,128)S(1)} %dynamic-slice_bitcast_fusion.2, pred[512,1024]{1,0:T(8,128)(4,1)S(1)} %broadcast_compare_fusion.6), kind=kLoop, calls=%fused_computation.14.clone.1 | loop fusion | flops 37748736 | bytes 63488000 | tf_op jit(solution)/shard_map/while/body/eval_jaxpr/convert_element_type | solution.py:95
  362.1 28.8 %dynamic_update_slice.19 = f32[2,512,12,64]{1,0,3,2:T(2,128)} dynamic-update-slice(f32[2,512,12,64]{1,0,3,2:T(2,128)} %get-tuple-element.512, f32[1,512,12,64]{1,0,3,2:T(1,128)S(1)} %copy.132, s32[]{:T(128)} %get-tuple-element.509, s32[]{:T(128)} %constant.71.clone.1..sunk.1, s32[]{:T(128)} %constant.71.clone.1..sunk.1, s32[]{:T(128)} %constant.71.clone.1..sunk.1) | dynamic-update-slice | bytes 3145732 | tf_op jit(solution)/shard_map/while/body/jit(dynamic_update_index_in_dim)/dynamic_update_slice | solution.py:67
  399.9 13.4 %bitcast_add_fusion.5 = f32[1024,12,64]{0,2,1:T(8,128)} fusion(f32[1024,12,64]{0,2,1:T(8,128)} %get-tuple-element.511, f32[12,512,1024]{2,1,0:T(8,128)} %fusion.125, f32[12,512]{1,0:T(8,128)S(1)} %dynamic-slice_bitcast_fusion.2, pred[512,1024]{1,0:T(8,128)(4,1)S(1)} %copy-done.7, pred[]{:T(512)S(6)} %compare.3, ...), kind=kOutput, calls=%fused_computation.20.clone.1 | convolution fusion | flops 832045056 | bytes 32800772 | tf_op jit(solution)/shard_map/while/body/eval_jaxpr/hqk,qhe->khe/dot_general | solution.py:83
  414.6 11.4 %fusion.125 = f32[12,512,1024]{2,1,0:T(8,128)} fusion(bf16[1024,12,64]{0,2,1:T(8,128)(2,1)S(1)} %get-tuple-element.531, bf16[1024,12,64]{0,2,1:T(8,128)(2,1)} %get-tuple-element.529, s32[]{:T(128)S(6)} %select_n.81), kind=kOutput, calls=%fused_computation.28.clone.1 | convolution fusion | flops 805306368 | bytes 27525124 | tf_op jit(solution)/shard_map/while/body/eval_jaxpr/qhe,khe->hqk/dot_general | solution.py:44
  426.4 18.3 %multiply_reduce_fusion.11 = (f32[12,512]{1,0:T(8,128)S(1)}, f32[12,512,1024]{2,1,0:T(8,128)}) fusion(f32[12,512,1024]{2,1,0:T(8,128)} %fusion.125, f32[12,512]{1,0:T(8,128)S(1)} %dynamic-slice_bitcast_fusion.2, pred[512,1024]{1,0:T(8,128)(4,1)S(1)} %broadcast_compare_fusion.6, bf16[1024,12,64]{0,2,1:T(8,128)(2,1)} %get-tuple-element.534, ...), kind=kOutput, calls=%fused_computation.15.clone.1 | convolution fusion | flops 836757504 | bytes 53264388 | tf_op jit(solution)/shard_map/while/body/eval_jaxpr/qhe,khe->hqk/dot_general | solution.py:89
  444.7 21.2 %multiply_convert_fusion.5 = bf16[12,512,1024]{2,1,0:T(8,128)(2,1)} fusion(f32[12,512,1024]{2,1,0:T(8,128)} %get-tuple-element.456, f32[12,512,1024]{2,1,0:T(8,128)} %fusion.125, f32[12,512]{1,0:T(8,128)S(1)} %get-tuple-element.457, f32[12,512]{1,0:T(8,128)S(1)} %dynamic-slice_bitcast_fusion.2, pred[512,1024]{1,0:T(8,128)(4,1)S(1)} %broadcast_compare_fusion.6), kind=kLoop, calls=%fused_computation.14.clone.1 | loop fusion | flops 37748736 | bytes 63488000 | tf_op jit(solution)/shard_map/while/body/eval_jaxpr/convert_element_type | solution.py:95
  478.6 28.7 %dynamic_update_slice.19 = f32[2,512,12,64]{1,0,3,2:T(2,128)} dynamic-update-slice(f32[2,512,12,64]{1,0,3,2:T(2,128)} %get-tuple-element.512, f32[1,512,12,64]{1,0,3,2:T(1,128)S(1)} %copy.132, s32[]{:T(128)} %get-tuple-element.509, s32[]{:T(128)} %constant.71.clone.1..sunk.1, s32[]{:T(128)} %constant.71.clone.1..sunk.1, s32[]{:T(128)} %constant.71.clone.1..sunk.1) | dynamic-update-slice | bytes 3145732 | tf_op jit(solution)/shard_map/while/body/jit(dynamic_update_index_in_dim)/dynamic_update_slice | solution.py:67
  517.1 14.2 %bitcast_add_fusion.5 = f32[1024,12,64]{0,2,1:T(8,128)} fusion(f32[1024,12,64]{0,2,1:T(8,128)} %get-tuple-element.511, f32[12,512,1024]{2,1,0:T(8,128)} %fusion.125, f32[12,512]{1,0:T(8,128)S(1)} %dynamic-slice_bitcast_fusion.2, pred[512,1024]{1,0:T(8,128)(4,1)S(1)} %copy-done.7, pred[]{:T(512)S(6)} %compare.3, ...), kind=kOutput, calls=%fused_computation.20.clone.1 | convolution fusion | flops 832045056 | bytes 32800772 | tf_op jit(solution)/shard_map/while/body/eval_jaxpr/hqk,qhe->khe/dot_general | solution.py:83
  593.9 46.2 %reduce-scatter.5.cloned.1.call-done = bf16[192,2304]{1,0:T(8,128)(2,1)} async-done(((bf16[768,2304]{1,0:T(8,128)(2,1)}), bf16[192,2304]{1,0:T(8,128)(2,1)}) %reduce-scatter.5.cloned.1.call-update) | async-done | bytes 884752 | tf_op jit(solution)/shard_map/reduce_scatter | solution.py:260
  661.1 15.5 %all-reduce.21 = (bf16[768]{0:T(1024)(128)(2,1)S(1)}, bf16[2304]{0:T(1024)(128)(2,1)S(1)}, bf16[768]{0:T(1024)(128)(2,1)S(1)}, bf16[3072]{0:T(1024)(128)(2,1)S(1...) all-reduce(bf16[768]{0:T(1024)(128)(2,1)S(1)} %dynamic-update-slice, ...), channel_id=1, replica_groups=mesh['dp'=8,'fsdp'=4] {'fsdp'}, use_global_device_ids=true, to_apply=%add.8 | all-reduce | flops 10880 | bytes 43520
  677.4 14.4 %all-reduce.19 = (bf16[576]{0:T(1024)(128)(2,1)S(1)}, bf16[192]{0:T(256)(128)(2,1)S(1)}, bf16[768]{0:T(1024)(128)(2,1)S(1)}, bf16[192]{0:T(256)(128)(2,1)S(1)}, ...) all-reduce(bf16[576]{0:T(1024)(128)(2,1)S(1)} %dynamic-slice.10, ...), channel_id=1, replica_groups=mesh['dp'=8,'fsdp'=4] {'dp'}, use_global_device_ids=true, to_apply=%region_27.28 | all-reduce | flops 2528 | bytes 10112 | tf_op jit(solution)/shard_map/psum | solution.py:305
  723.3 61.2 %all-gather.16.cloned.1.call-done = bf16[1536,2304]{1,0:T(8,128)(2,1)} async-done(((bf16[192,2304]{1,0:T(8,128)(2,1)}), bf16[1536,2304]{1,0:T(8,128)(2,1)}) %all-gather.16.cloned.1.call-update) | async-done | bytes 7077904 | tf_op jit(solution)/shard_map/all_gather | solution.py:304
  (400 shorter events, 311.8 us)
Async XLA Ops:
  7.3 26.5 %copy-start.35 = (bf16[1024,768]{1,0:T(8,128)(2,1)S(1)}, bf16[1024,768]{1,0:T(8,128)(2,1)}, u32[]{:S(2)}) copy-start(bf16[1024,768]{1,0:T(8,128)(2,1)} %param.21) | copy-start | bytes 4718596
  7.3 52.9 %all-gather.8.cloned.1.call-start = ((), (), s32[]{:S(2)}) async-start(), calls=%async_computation.4 | async-start | bytes 4423680 | tf_op jit(solution)/shard_map/all_gather | solution.py:131
  8.0 160.2 %all-gather.10.cloned.1.call-start = ((), (), s32[]{:S(2)}) async-start(), calls=%async_computation.5 | async-start | bytes 1474560 | tf_op jit(solution)/shard_map/all_gather | solution.py:133
  8.8 163.8 %all-gather.12.cloned.1.call-start = ((), (), s32[]{:S(2)}) async-start(), calls=%async_computation.6 | async-start | bytes 5898240 | tf_op jit(solution)/shard_map/all_gather | solution.py:135
  9.5 201.4 %all-gather.14.cloned.1.call-start = ((), (), s32[]{:S(2)}) async-start(), calls=%async_computation.7 | async-start | bytes 5898240 | tf_op jit(solution)/shard_map/all_gather | solution.py:137
  10.1 583.1 %reduce-scatter.7.cloned.1.call-start = ((), (), s32[]{:S(2)}) async-start(), calls=%async_computation.9 | async-start | bytes 1474560 | tf_op jit(solution)/shard_map/reduce_scatter | solution.py:266
  33.7 26.4 %copy-start.57 = (f32[768]{0:T(1024)}, f32[768]{0:T(1024)S(1)}, u32[]{:S(2)}) copy-start(f32[768]{0:T(1024)S(1)} %convert_element_type.200) | copy-start | bytes 9220
  33.7 26.4 %copy-start.78 = (f32[768]{0:T(1024)}, f32[768]{0:T(1024)S(1)}, u32[]{:S(2)}) copy-start(f32[768]{0:T(1024)S(1)} %convert_element_type.201) | copy-start | bytes 9220
  34.6 25.6 %copy-start.13 = (bf16[1024,768]{0,1:T(8,128)(2,1)}, bf16[1024,768]{0,1:T(8,128)(2,1)S(1)}, u32[]{:S(2)}) copy-start(bf16[1024,768]{0,1:T(8,128)(2,1)S(1)} %copy.78) | copy-start | bytes 4718596
  34.9 31.6 %copy-start.55 = (f32[1024]{0:T(1024)}, f32[1024]{0:T(1024)S(1)}, u32[]{:S(2)}) copy-start(f32[1024]{0:T(1024)S(1)} %broadcast_multiply_fusion.3) | copy-start | bytes 12292
  35.3 31.1 %copy-start.59 = (f32[1024]{0:T(1024)}, f32[1024]{0:T(1024)S(1)}, u32[]{:S(2)}) copy-start(f32[1024]{0:T(1024)S(1)} %fusion.54) | copy-start | bytes 12292
  35.4 49.3 %copy-start.76 = (f32[64]{0:T(128)}, f32[64]{0:T(128)S(1)}, u32[]{:S(2)}) copy-start(f32[64]{0:T(128)S(1)} %convert_element_type.204) | copy-start | bytes 772
  35.4 49.3 %copy-start.70 = (f32[64]{0:T(128)}, f32[64]{0:T(128)S(1)}, u32[]{:S(2)}) copy-start(f32[64]{0:T(128)S(1)} %convert_element_type.206) | copy-start | bytes 772
  172.1 82.0 %copy-start.16 = (f32[1024,768]{0,1:T(8,128)}, f32[1024,768]{0,1:T(8,128)S(1)}, u32[]{:S(2)}) copy-start(f32[1024,768]{0,1:T(8,128)S(1)} %get-tuple-element.324) | copy-start | bytes 9437188
  172.9 38.0 %copy-start.68 = (pred[1024]{0:T(1024)(128)(4,1)S(1)}, pred[1024]{0:T(1024)(128)(4,1)}, u32[]{:S(2)}) copy-start(pred[1024]{0:T(1024)(128)(4,1)} %broadcast_compare_fusion.2) | copy-start | bytes 3076
  254.1 339.1 %reduce-scatter.9.cloned.1.call-start = ((), (), s32[]{:S(2)}) async-start(), calls=%async_computation.10 | async-start | bytes 5898240 | tf_op jit(solution)/shard_map/reduce_scatter | solution.py:272
  263.9 329.3 %reduce-scatter.11.cloned.1.call-start = ((), (), s32[]{:S(2)}) async-start(), calls=%async_computation.11 | async-start | bytes 5898240 | tf_op jit(solution)/shard_map/reduce_scatter | solution.py:278
  288.0 352.1 %reduce-scatter.5.cloned.1.call-start = ((), (), s32[]{:S(2)}) async-start(), calls=%async_computation.8 | async-start | bytes 4423680 | tf_op jit(solution)/shard_map/reduce_scatter | solution.py:260
  593.1 49.6 %copy-start.95 = (bf16[192]{0:T(256)(128)(2,1)S(1)}, bf16[192]{0:T(256)(128)(2,1)}, u32[]{:S(2)}) copy-start(bf16[192]{0:T(256)(128)(2,1)} %param.31) | copy-start | bytes 1156
  593.1 124.7 %all-reduce.25.cloned.1.call-start = ((), (), s32[]{:S(2)}) async-start(), calls=%async_computation.13 | async-start | bytes 5308416 | tf_op jit(solution)/shard_map/psum | solution.py:306
  593.8 190.7 %all-gather.16.cloned.1.call-start = ((), (), s32[]{:S(2)}) async-start(), calls=%async_computation.12 | async-start | bytes 7962624 | tf_op jit(solution)/shard_map/all_gather | solution.py:304
  659.7 37.6 %copy-start.23 = (bf16[1024,768]{0,1:T(8,128)(2,1)S(1)}, bf16[1024,768]{0,1:T(8,128)(2,1)}, u32[]{:S(2)}) copy-start(bf16[1024,768]{0,1:T(8,128)(2,1)} %copy.84) | copy-start | bytes 4718596
  659.7 37.6 %copy-start.62 = (f32[1024]{0:T(1024)S(1)}, f32[1024]{0:T(1024)}, u32[]{:S(2)}) copy-start(f32[1024]{0:T(1024)} %copy-done.61) | copy-start | bytes 12292
  659.7 37.6 %copy-start.69 = (pred[1024]{0:T(1024)(128)(4,1)S(1)}, pred[1024]{0:T(1024)(128)(4,1)}, u32[]{:S(2)}) copy-start(pred[1024]{0:T(1024)(128)(4,1)} %broadcast_compare_fusion.2) | copy-start | bytes 3076
  (87 other events, 475.9 us)
Sparse Core Ops, SparseCore 0:
  9.9 50.1 all-gather.7
  62.0 27.5 all-gather.9
  91.4 56.9 all-gather.11
  150.1 56.9 all-gather.13
  254.2 28.6 reduce-scatter.6
  285.8 56.9 reduce-scatter.8
  345.8 56.9 reduce-scatter.10
  593.2 46.7 reduce-scatter.4
  642.7 69.7 all-reduce.24
  713.9 70.6 all-gather.15
